TPU v7x, 32 devices: a whole 2x2x4 slice. The times are simulated.
32 devices in a mesh: dp: 8 (over y, x, core), seq: 4 (over z).
Axes of the slice: x: 2, y: 2, z: 4, core: 2. Of those that a mesh axis runs over, the one named last changes fastest.
Arguments:
- hidden: bfloat16 [8192, 1792], P(('dp', 'seq')), may hold values from -12.75 to 12.75
- depths: int32 [8192], P(('dp', 'seq')), may hold values from 1 to 3, as said below
- packed_slot_index: int32 [8192], P(('dp', 'seq')), may hold values from -1 to 511, as said below
- value_weight: bfloat16 [1792, 1024], P('dp'), may hold values from -0.125 to 0.125
- output_weight: bfloat16 [1024, 1792], P('dp'), may hold values from -0.1875 to 0.1875
- adapter_down_factor: bfloat16 [1792, 128], P('dp'), may hold values from -0.125 to 0.125
- adapter_up_factor: bfloat16 [1024, 128], P('dp'), may hold values from -0.5 to 0.5
- before_norm_gain: float32 [1792], replicated, may hold values from 0.1 to 1.9
- after_norm_gain: float32 [1792], replicated, may hold values from 0.1 to 1.9
- cotangent: bfloat16 [4096, 1792], P(('dp', 'seq')), may hold values from -6 to 6
Outputs:
- looped: bfloat16 [4096, 1792], P(('dp', 'seq'))
- grad_hidden: bfloat16 [8192, 1792], P(('dp', 'seq'))
- down_factor_gradient: float32 [1792, 128], P('dp', 'seq')
- up_factor_gradient: float32 [1024, 128], P('dp', 'seq')
Inputs may be any that keep to these rules, and one draw needn't show every extreme that they name: `depths`: of the 1024 tokens of one dp index exactly 512 have depth 2 or 3, and all 256 tokens of one seq index are among them. -1 exactly where depths is 1. Over the tokens of one dp index with depth 2 or 3 the slots are a permutation of 0 to 511; packed_slot_index // 128 is the seq index that holds the token's packed row. At most 64 tokens of one device have slots of one seq index, and exactly 64 do in every dp index.
All inputs are finite; a program needn't handle non-finite values.
Results may differ from a plain program's by a relative error of at most 0.01.
Values may be sent and summed in bfloat16 or wider, within the bound.
A program may use at most 64 MiB of HBM per device.

v0:
```python
import math
import jax
import jax.numpy as jnp
from jax import lax
from jax.sharding import PartitionSpec as P

epsilon = 1e-06


def contract_final_axis(left, right):
    return lax.dot_general(
        left, right, (((1,), (1,)), ((), ())), preferred_element_type=jnp.float32
    )


def contract_first(left, right):
    return lax.dot_general(
        left, right, (((0,), (0,)), ((), ())), preferred_element_type=jnp.float32
    )


def layer_forward(
    input_rows,
    cotangent_rows,
    value_weight,
    output_weight,
    adapter_down_factor,
    adapter_up_factor,
    before_norm_gain,
    after_norm_gain,
):
    x_float = input_rows.astype(jnp.float32)
    inv_pre = lax.rsqrt(jnp.mean(x_float * x_float, axis=-1, keepdims=True) + epsilon)
    whitened = x_float * inv_pre
    normalized_rows = (whitened * before_norm_gain).astype(jnp.bfloat16)
    rank_reduced = jnp.dot(
        normalized_rows, adapter_down_factor, preferred_element_type=jnp.float32
    ).astype(jnp.bfloat16)
    projected_rows = (
        jnp.dot(normalized_rows, value_weight, preferred_element_type=jnp.float32)
        + contract_final_axis(rank_reduced, adapter_up_factor)
    ).astype(jnp.bfloat16)
    mixed_out = jnp.dot(projected_rows, output_weight, preferred_element_type=jnp.float32)
    inv_post = lax.rsqrt(jnp.mean(mixed_out * mixed_out, axis=-1, keepdims=True) + epsilon)
    shaped = mixed_out * inv_post
    looped = (x_float + shaped * after_norm_gain).astype(jnp.bfloat16)
    cot_float = cotangent_rows.astype(jnp.float32)
    grad_shaped = cot_float * after_norm_gain
    grad_mixed = (
        inv_post * (grad_shaped - shaped * jnp.mean(grad_shaped * shaped, axis=-1, keepdims=True))
    ).astype(jnp.bfloat16)
    value_gradient = contract_final_axis(grad_mixed, output_weight).astype(jnp.bfloat16)
    low_rank_gradient = jnp.dot(
        value_gradient, adapter_up_factor, preferred_element_type=jnp.float32
    ).astype(jnp.bfloat16)
    normalized_gradient = contract_final_axis(value_gradient, value_weight) + contract_final_axis(
        low_rank_gradient, adapter_down_factor
    )
    grad_white = normalized_gradient * before_norm_gain
    gradient_rows = (
        cot_float
        + inv_pre
        * (grad_white - whitened * jnp.mean(grad_white * whitened, axis=-1, keepdims=True))
    ).astype(jnp.bfloat16)
    down_factor_gradient = contract_first(normalized_rows, low_rank_gradient)
    up_factor_gradient = contract_first(value_gradient, rank_reduced)
    return (looped, gradient_rows, down_factor_gradient, up_factor_gradient)


def body(
    hidden,
    depths,
    packed_slot_index,
    value_weight,
    output_weight,
    adapter_down_factor,
    adapter_up_factor,
    before_norm_gain,
    after_norm_gain,
    cotangent,
):
    seq_count = lax.axis_size("seq")
    own_index = lax.axis_index("seq")
    tok_count = hidden.shape[0]
    act_rows = cotangent.shape[0]
    value_full, out_full, down_full, up_full = (
        lax.all_gather(value_weight, "dp", axis=0, tiled=True),
        lax.all_gather(output_weight, "dp", axis=0, tiled=True),
        lax.all_gather(adapter_down_factor, "dp", axis=0, tiled=True),
        lax.all_gather(adapter_up_factor, "dp", axis=0, tiled=True),
    )
    depth_all, slot_all = (
        lax.all_gather(depths, "seq", axis=0, tiled=True),
        lax.all_gather(packed_slot_index, "seq", axis=0, tiled=True),
    )
    active_all = depth_all >= 2
    dest_all = jnp.where(active_all, slot_all // act_rows, -1)
    pos_all = jnp.where(active_all, slot_all % act_rows, 0)
    mine = active_all & (dest_all == own_index)
    active = depths >= 2
    zero_row = jnp.zeros((), jnp.bfloat16)
    rows_all = lax.all_gather(hidden, "seq", axis=0, tiled=True)
    source = (
        jnp.zeros((act_rows,), jnp.int32)
        .at[jnp.where(mine, pos_all, act_rows)]
        .set(jnp.arange(seq_count * tok_count, dtype=jnp.int32), mode="drop")
    )
    packed = jnp.take(rows_all, source, axis=0)
    looped, gradient_rows, down_factor_gradient, up_factor_gradient = layer_forward(
        packed,
        cotangent,
        value_full,
        out_full,
        down_full,
        up_full,
        before_norm_gain,
        after_norm_gain,
    )
    grads_all = lax.all_gather(gradient_rows, "seq", axis=0, tiled=True)
    picked = jnp.take(grads_all, jnp.maximum(packed_slot_index, 0), axis=0)
    grad_hidden = jnp.where(active[:, None], picked, zero_row)
    grad_scale = 1.0 / math.sqrt(seq_count * act_rows * lax.axis_size("dp"))
    down_term = down_factor_gradient * grad_scale
    up_term = up_factor_gradient * grad_scale
    down_mid, up_mid = (
        lax.psum_scatter(
            down_term.astype(jnp.bfloat16), "seq", scatter_dimension=1, tiled=True
        ).astype(jnp.float32),
        lax.psum_scatter(
            up_term.astype(jnp.bfloat16), "seq", scatter_dimension=1, tiled=True
        ).astype(jnp.float32),
    )
    down_sum, up_sum = (
        lax.psum_scatter(down_mid, "dp", scatter_dimension=0, tiled=True),
        lax.psum_scatter(up_mid, "dp", scatter_dimension=0, tiled=True),
    )
    return (looped, grad_hidden, down_sum, up_sum)


def solution(mesh):
    placed = (
        P(("dp", "seq"), None),
        P(("dp", "seq")),
        P(("dp", "seq")),
        P("dp", None),
        P("dp", None),
        P("dp", None),
        P("dp", None),
        P(),
        P(),
        P(("dp", "seq"), None),
    )
    return jax.shard_map(
        body,
        mesh=mesh,
        in_specs=placed,
        out_specs=(P(("dp", "seq"), None), P(("dp", "seq"), None), P("dp", "seq"), P("dp", "seq")),
        check_vma=False,
    )
```

profile of v0, /device:TPU:0, one launch (start us, length us, event | category | flops | bytes accessed | tf_op | source)
XLA Modules:
  0.0 329.3 jit_solution(13722843027043391828)
XLA Ops:
  7.2 0.0 copy-start.2
  7.2 0.0 all-gather.7.cloned.1.call-start
  7.2 0.7 all-gather.7.cloned.1.call-update
  7.9 0.0 all-gather.9.cloned.1.call-start
  8.0 0.7 all-gather.9.cloned.1.call-update
  8.7 0.0 all-gather.11.cloned.1.call-start
  8.7 0.7 all-gather.11.cloned.1.call-update
  9.4 0.0 reduce-scatter.7.cloned.1.call-start
  9.4 12.8 %all-gather = s32[4,1,256]{2,1,0:T(1,128)S(1)} all-gather(s32[1,1,256]{2,1,0:T(1,128)} %bitcast.21), channel_id=1, replica_groups=mesh['dp'=8,'seq'=4] {'seq'}, dimensions={0}, use_global_device_ids=true | all-gather | bytes 5120 | tf_op jit(solution)/shard_map/all_gather | solution.py:93
  22.3 8.1 %all-gather.1 = s32[4,1,256]{2,1,0:T(1,128)S(1)} all-gather(s32[1,1,256]{2,1,0:T(1,128)} %bitcast.20), channel_id=1, replica_groups=mesh['dp'=8,'seq'=4] {'seq'}, dimensions={0}, use_global_device_ids=true | all-gather | bytes 5120 | tf_op jit(solution)/shard_map/all_gather | solution.py:94
  30.4 4.3 %scatter_custom_fusion = s32[128]{0:T(128)S(1)} fusion(s32[1024]{0:T(1024)S(1)} %compare_select_fusion, s32[1024]{0:T(1024)S(1)} %iota.3, s32[]{:T(128)} %constant.69.clone.1), kind=kCustom, calls=%fused_computation.69 | custom fusion | bytes 516 | tf_op jit(solution)/shard_map/scatter | solution.py:106
  34.8 9.5 %all_gather.29 = bf16[1024,128]{1,0:T(8,128)(2,1)S(1)} all-gather(bf16[128,128]{1,0:T(8,128)(2,1)} %param.16), channel_id=1, replica_groups=mesh['dp'=8,'seq'=4] {'dp'}, dimensions={0}, use_global_device_ids=true | all-gather | bytes 294912 | tf_op jit(solution)/shard_map/all_gather | solution.py:90
  44.3 9.5 %all_gather.28 = bf16[1792,128]{1,0:T(8,128)(2,1)S(1)} all-gather(bf16[224,128]{1,0:T(8,128)(2,1)} %param.15), channel_id=1, replica_groups=mesh['dp'=8,'seq'=4] {'dp'}, dimensions={0}, use_global_device_ids=true | all-gather | bytes 516096 | tf_op jit(solution)/shard_map/all_gather | solution.py:89
  53.8 30.7 %all-gather.7.cloned.1.call-done = bf16[1024,1792]{1,0:T(8,128)(2,1)} async-done(((bf16[256,1792]{1,0:T(8,128)(2,1)}), bf16[1024,1792]{1,0:T(8,128)(2,1)}) %all-gather.7.cloned.1.call-update) | async-done | bytes 3670032 | tf_op jit(solution)/shard_map/all_gather | solution.py:102
  84.5 3.8 %gather_fusion = bf16[128,1792]{1,0:T(8,128)(2,1)S(1)} fusion(bf16[1024,1792]{1,0:T(8,128)(2,1)} %all-gather.7.cloned.1.call-done, s32[1024]{0:T(1024)S(1)} %pad_clamp_fusion.1), kind=kCustom, calls=%fused_computation | custom fusion | bytes 918016 | tf_op jit(solution)/shard_map/jit(_take)/gather | solution.py:108
  88.4 0.3 fusion.18
  88.7 0.0 copy-done.2
  88.7 0.4 convolution_convert_fusion.1
  89.0 30.5 %all-gather.9.cloned.1.call-done = bf16[1792,1024]{1,0:T(8,128)(2,1)} async-done(((bf16[224,1024]{1,0:T(8,128)(2,1)}), bf16[1792,1024]{1,0:T(8,128)(2,1)}) %all-gather.9.cloned.1.call-update) | async-done | bytes 3670032 | tf_op jit(solution)/shard_map/all_gather | solution.py:87
  119.5 2.7 fusion.37
  122.3 0.0 copy-start
  122.3 0.0 copy-start.1
  122.3 33.7 %all-gather.11.cloned.1.call-done = bf16[1024,1792]{1,0:T(8,128)(2,1)} async-done(((bf16[128,1792]{1,0:T(8,128)(2,1)}), bf16[1024,1792]{1,0:T(8,128)(2,1)}) %all-gather.11.cloned.1.call-update) | async-done | bytes 3670032 | tf_op jit(solution)/shard_map/all_gather | solution.py:88
  156.0 2.9 multiply_reduce_fusion
  158.9 0.0 copy-done
  158.9 0.0 copy-done.1
  158.9 1.1 fusion.10
  160.0 3.4 %convolution_convert_fusion = bf16[128,1024]{1,0:T(8,128)(2,1)S(1)} fusion(bf16[1024,1792]{1,0:T(8,128)(2,1)} %all-gather.11.cloned.1.call-done, bf16[128,1792]{1,0:T(8,128)(2,1)S(1)} %copy-done, f32[128,1792]{1,0:T(8,128)S(1)} %get-tuple-element.7, f32[128]{0:T(128)S(1)} %broadcast_multiply_fusion.1, f32[1792]{0:T(1024)S(1)} %copy-done.1, ...), kind=kOutput, calls=%fused_computation.15 | convolution fusion | flops 471498752 | bytes 5316608 | tf_op jit(solution)/shard_map/dot_general | solution.py:11
  163.4 0.2 convolution_convert_fusion.2
  163.6 1.2 fusion.1
  164.8 0.0 reduce-scatter.7.cloned.1.call-update
  164.8 0.0 reduce-scatter.9.cloned.1.call-start
  164.9 1.0 fusion.6
  165.8 0.0 reduce-scatter.9.cloned.1.call-update
  165.8 0.0 reduce-scatter.13.cloned.1.call-start
  165.9 3.4 %fusion.39 = f32[128,1792]{1,0:T(8,128)S(1)} fusion(bf16[128,1024]{1,0:T(8,128)(2,1)S(1)} %convolution_convert_fusion, bf16[1792,1024]{1,0:T(8,128)(2,1)} %all-gather.9.cloned.1.call-done), kind=kOutput, calls=%fused_computation.72 | convolution fusion | flops 469762048 | bytes 4849664 | tf_op jit(solution)/shard_map/dot_general | solution.py:11
  169.3 0.0 copy-start.3
  169.3 0.0 copy-start.4
  169.3 0.4 fusion.15
  169.8 16.2 %reduce-scatter.7.cloned.1.call-done = bf16[1792,32]{0,1:T(8,128)(2,1)} async-done(((bf16[1792,128]{0,1:T(8,128)(2,1)}), bf16[1792,32]{0,1:T(8,128)(2,1)}) %reduce-scatter.7.cloned.1.call-update) | async-done | bytes 114704 | tf_op jit(solution)/shard_map/reduce_scatter | solution.py:126
  186.0 2.0 copy.14
  188.0 0.0 reduce-scatter.13.cloned.1.call-update
  188.0 0.0 all-gather.13.cloned.1.call-start
  188.1 1.3 fusion.13
  189.4 0.0 all-gather.13.cloned.1.call-update
  189.4 0.0 reduce-scatter.11.cloned.1.call-start
  189.5 0.0 copy-done.3
  189.5 0.0 copy-done.4
  189.6 16.7 %reduce-scatter.9.cloned.1.call-done = bf16[1024,32]{0,1:T(8,128)(2,1)} async-done(((bf16[1024,128]{0,1:T(8,128)(2,1)}), bf16[1024,32]{0,1:T(8,128)(2,1)}) %reduce-scatter.9.cloned.1.call-update) | async-done | bytes 65552 | tf_op jit(solution)/shard_map/reduce_scatter | solution.py:129
  206.3 1.5 convert_element_type.55
  207.8 0.0 reduce-scatter.11.cloned.1.call-update
  207.8 35.8 %reduce-scatter.13.cloned.1.call-done = f32[224,32]{1,0:T(8,128)} async-done(((f32[1792,32]{1,0:T(8,128)}), f32[224,32]{1,0:T(8,128)}) %reduce-scatter.13.cloned.1.call-update) | async-done | bytes 28688
  243.6 1.6 copy.15
  245.2 41.4 %all-gather.13.cloned.1.call-done = bf16[512,1792]{1,0:T(8,128)(2,1)} async-done(((bf16[128,1792]{1,0:T(8,128)(2,1)}), bf16[512,1792]{1,0:T(8,128)(2,1)}) %all-gather.13.cloned.1.call-update) | async-done | bytes 1835024 | tf_op jit(solution)/shard_map/all_gather | solution.py:119
  286.6 3.9 %gather_fusion.1 = bf16[256,1792]{1,0:T(8,128)(2,1)S(1)} fusion(bf16[512,1792]{1,0:T(8,128)(2,1)} %all-gather.13.cloned.1.call-done, s32[1024]{0:T(1024)S(1)} %pad_clamp_fusion), kind=kCustom, calls=%fused_computation.1 | custom fusion | bytes 1836032 | tf_op jit(solution)/shard_map/jit(_take)/gather | solution.py:120
  290.5 1.1 select_select_fusion
  291.6 30.8 %reduce-scatter.11.cloned.1.call-done = f32[128,32]{0,1:T(8,128)} async-done(((f32[1024,32]{0,1:T(8,128)}), f32[128,32]{0,1:T(8,128)}) %reduce-scatter.11.cloned.1.call-update) | async-done | bytes 16400 | tf_op jit(solution)/shard_map/reduce_scatter | solution.py:135
  (15 shorter events, 0.1 us)
Async XLA Ops:
  7.2 81.5 %copy-start.2 = (f32[1792]{0:T(1024)S(1)}, f32[1792]{0:T(1024)}, u32[]{:S(2)}) copy-start(f32[1792]{0:T(1024)} %param.17) | copy-start | bytes 21508
  7.2 77.3 %all-gather.7.cloned.1.call-start = ((), (), s32[]{:S(2)}) async-start(), calls=%async_computation.4 | async-start | bytes 4587520 | tf_op jit(solution)/shard_map/all_gather | solution.py:102
  7.9 111.6 %all-gather.9.cloned.1.call-start = ((), (), s32[]{:S(2)}) async-start(), calls=%async_computation.5 | async-start | bytes 4128768 | tf_op jit(solution)/shard_map/all_gather | solution.py:87
  8.7 147.3 %all-gather.11.cloned.1.call-start = ((), (), s32[]{:S(2)}) async-start(), calls=%async_computation.6 | async-start | bytes 4128768 | tf_op jit(solution)/shard_map/all_gather | solution.py:88
  9.4 176.6 %reduce-scatter.7.cloned.1.call-start = ((), (), s32[]{:S(2)}) async-start(), calls=%async_computation.8 | async-start | bytes 573440 | tf_op jit(solution)/shard_map/reduce_scatter | solution.py:126
  122.3 36.7 %copy-start = (bf16[128,1792]{1,0:T(8,128)(2,1)S(1)}, bf16[128,1792]{1,0:T(8,128)(2,1)}, u32[]{:S(2)}) copy-start(bf16[128,1792]{1,0:T(8,128)(2,1)} %param.19) | copy-start | bytes 1376260
  122.3 36.6 %copy-start.1 = (f32[1792]{0:T(1024)S(1)}, f32[1792]{0:T(1024)}, u32[]{:S(2)}) copy-start(f32[1792]{0:T(1024)} %param.18) | copy-start | bytes 21508
  164.8 41.5 %reduce-scatter.9.cloned.1.call-start = ((), (), s32[]{:S(2)}) async-start(), calls=%async_computation.9 | async-start | bytes 327680 | tf_op jit(solution)/shard_map/reduce_scatter | solution.py:129
  165.8 77.8 %reduce-scatter.13.cloned.1.call-start = ((), (), s32[]{:S(2)}) async-start(), calls=%async_computation.11 | async-start | bytes 1032192
  169.3 20.2 %copy-start.3 = (s32[256]{0:T(256)S(1)}, s32[256]{0:T(256)}, u32[]{:S(2)}) copy-start(s32[256]{0:T(256)} %param.12) | copy-start | bytes 3076
  169.3 20.3 %copy-start.4 = (s32[256]{0:T(256)S(1)}, s32[256]{0:T(256)}, u32[]{:S(2)}) copy-start(s32[256]{0:T(256)} %param.11) | copy-start | bytes 3076
  188.0 98.6 %all-gather.13.cloned.1.call-start = ((), (), s32[]{:S(2)}) async-start(), calls=%async_computation.7 | async-start | bytes 2293760 | tf_op jit(solution)/shard_map/all_gather | solution.py:119
  189.4 133.0 %reduce-scatter.11.cloned.1.call-start = ((), (), s32[]{:S(2)}) async-start(), calls=%async_computation.10 | async-start | bytes 147456 | tf_op jit(solution)/shard_map/reduce_scatter | solution.py:135
Sparse Core Ops, SparseCore 0:
  9.6 74.8 all-gather.6
  86.4 33.0 all-gather.8
  121.4 34.5 all-gather.10
  164.9 20.9 reduce-scatter.6
  188.2 18.0 reduce-scatter.8
  209.9 33.6 reduce-scatter.12
  245.2 41.3 all-gather.12
  290.2 32.2 reduce-scatter.10
where the time goes:
time: 330 us; the launch traced here: 329 us
  waiting for transfers between devices  238 us (72%)
  blocking collectives  39.9 us (12%)
  local copies, waits for them, and re-layouts  15.7 us (5%)
  matrix products  15.5 us (5%)
  between operations  14.3 us (4%)
  other arithmetic  5.43 us (2%)
    all_gather x1, waiting for transfers between devices, body(): grads_all = lax.all_gather(gradient_rows, 'seq', axis=0, tiled=True)  41.4 us
    unnamed x9, waiting for transfers between devices  38 us
    all_gather x1, waiting for transfers between devices, body(): lax.all_gather(output_weight, 'dp', axis=0, tiled=True)  33.7 us
    reduce_scatter x1, waiting for transfers between devices, body(): lax.psum_scatter(up_mid, 'dp', scatter_dimension=0, tiled=True)  30.8 us
    all_gather x1, waiting for transfers between devices, body(): rows_all = lax.all_gather(hidden, 'seq', axis=0, tiled=True)  30.7 us
    all_gather x1, waiting for transfers between devices, body(): lax.all_gather(value_weight, 'dp', axis=0, tiled=True)  30.5 us
    reduce_scatter x1, waiting for transfers between devices, body(): lax.psum_scatter(up_term.astype(jnp.bfloat16), 'seq', scatter_dimension=1...  16.7 us
    reduce_scatter x1, waiting for transfers between devices, body(): lax.psum_scatter(down_term.astype(jnp.bfloat16), 'seq', scatter_dimension...  16.2 us
  transfers between devices with their start and end apart: 8, of which 8 were waited for; matrix products, arithmetic and copies ran while one was open for 8% of the time, Pallas kernels for 0%

commit v1 on v0

--- a/solution.py
+++ b/solution.py
@@ -5,6 +5,28 @@
 from jax.sharding import PartitionSpec as P
 
 epsilon = 1e-06
+
+
+def in_order(blocks, dim):
+    shape = list(blocks.shape[1:])
+    shape[dim] *= blocks.shape[0]
+    return jnp.moveaxis(blocks, 0, dim).reshape(shape)
+
+
+def doubled(array, axis):
+    size = lax.axis_size(axis)
+    blocks = array[None]
+    for level in range(size.bit_length() - 1):
+        bit = 1 << level
+        received = lax.ppermute(blocks, axis, [(i, i ^ bit) for i in range(size)])
+        both = jnp.stack([blocks, received])
+        upper = lax.axis_index(axis) >> level & 1
+        blocks = jnp.where(upper == 0, both, both[::-1]).reshape(-1, *array.shape)
+    return blocks
+
+
+def gather_by_bits(array, axis, dim):
+    return in_order(doubled(array, axis), dim)
 
 
 def contract_final_axis(left, right):
@@ -85,7 +107,7 @@
     act_rows = cotangent.shape[0]
     value_full, out_full, down_full, up_full = (
         lax.all_gather(value_weight, "dp", axis=0, tiled=True),
-        lax.all_gather(output_weight, "dp", axis=0, tiled=True),
+        gather_by_bits(output_weight, "dp", 0),
         lax.all_gather(adapter_down_factor, "dp", axis=0, tiled=True),
         lax.all_gather(adapter_up_factor, "dp", axis=0, tiled=True),
     )

time: 330 us -> 296 us (0.90)
  waiting for transfers between devices: 238 us -> 183 us
  blocking collectives: 39.9 us -> 49.7 us
  other arithmetic: 5.43 us -> 11.7 us
  starting transfers between devices: 0.32 us -> 5.56 us
    all_gather x1 -> x0, waiting for transfers between devices: 33.7 us -> none  [body(): lax.all_gather(output_weight, 'dp', axis=0, tiled=True)]
    all_gather x1, waiting for transfers between devices: 30.7 us -> 0.01 us  [body(): rows_all = lax.all_gather(hidden, 'seq', axis=0, tiled=True)]
    ppermute x0 -> x3, waiting for transfers between devices: none -> 22.3 us  [doubled(): received = lax.ppermute(blocks, axis, [(i, i ^ bit) for i in range(size)])]
    all_gather x1, waiting for transfers between devices: 30.5 us -> 18.3 us  [body(): lax.all_gather(value_weight, 'dp', axis=0, tiled=True)]
    all_gather x1, blocking collectives: 9.53 us -> 20.3 us  [body(): lax.all_gather(adapter_up_factor, 'dp', axis=0, tiled=True)]
    ppermute x0 -> x3, starting transfers between devices: none -> 5.28 us  [doubled(): received = lax.ppermute(blocks, axis, [(i, i ^ bit) for i in range(size)])]
    another operation x0 -> x4, other arithmetic: none -> 3.36 us  [doubled(): both = jnp.stack([blocks, received])]
    unnamed x9 -> x8, waiting for transfers between devices: 38 us -> 37.3 us
  transfers between devices with their start and end apart: 8 -> 10, of which waited for: 8 -> 8; matrix products, arithmetic and copies ran while one was open for 8% -> 11% of each run, Pallas kernels for 0% -> 0%
where the time goes in v1:
time: 296 us
  waiting for transfers between devices  183 us (62%)
  blocking collectives  49.7 us (17%)
  local copies, waits for them, and re-layouts  15.7 us (5%)
  matrix products  15.6 us (5%)
  between operations  14.3 us (5%)
  other arithmetic  11.7 us (4%)
  starting transfers between devices  5.56 us (2%)
    all_gather x1, waiting for transfers between devices, body(): grads_all = lax.all_gather(gradient_rows, 'seq', axis=0, tiled=True)  41.3 us
    unnamed x8, waiting for transfers between devices  37.3 us
    reduce_scatter x1, waiting for transfers between devices, body(): lax.psum_scatter(up_mid, 'dp', scatter_dimension=0, tiled=True)  30.8 us
    ppermute x3, waiting for transfers between devices, doubled(): received = lax.ppermute(blocks, axis, [(i, i ^ bit) for i in range(size)])  22.3 us
    all_gather x1, blocking collectives, body(): lax.all_gather(adapter_up_factor, 'dp', axis=0, tiled=True)  20.3 us
    all_gather x1, waiting for transfers between devices, body(): lax.all_gather(value_weight, 'dp', axis=0, tiled=True)  18.3 us
    reduce_scatter x1, waiting for transfers between devices, body(): lax.psum_scatter(up_term.astype(jnp.bfloat16), 'seq', scatter_dimension=1...  16.7 us
    reduce_scatter x1, waiting for transfers between devices, body(): lax.psum_scatter(down_term.astype(jnp.bfloat16), 'seq', scatter_dimension...  16.3 us
  transfers between devices with their start and end apart: 10, of which 8 were waited for; matrix products, arithmetic and copies ran while one was open for 11% of the time, Pallas kernels for 0%

profile of v1, /device:TPU:0, one launch (start us, length us, event | category | flops | bytes accessed | tf_op | source)
XLA Modules:
  0.0 295.6 jit_solution(17292823335135200075)
XLA Ops:
  7.2 0.0 all-gather.6.cloned.1.call-start
  7.2 0.7 all-gather.6.cloned.1.call-update
  7.9 0.0 all-gather.8.cloned.1.call-start
  7.9 0.7 all-gather.8.cloned.1.call-update
  8.6 0.0 reduce-scatter.7.cloned.1.call-start
  8.7 0.5 collective-permute-start
  9.2 1.7 collective-permute-done
  10.9 1.1 pad_maximum_fusion.2
  12.0 0.2 fusion.21
  12.1 2.9 collective-permute-start.1
  15.1 20.7 %collective-permute-done.1 = bf16[2,128,1792]{2,1,0:T(8,128)(2,1)S(1)} collective-permute-done((bf16[2,128,1792]{2,1,0:T(8,128)(2,1)S(1)}, bf16[2,128,1792]{2,1,0:T(8,128)(2,1)S(1)}, u32[]{:S(2)}, u32[]{:S(2)}) %collective-permute-start.1) | collective-permute-done | bytes 917536 | tf_op jit(solution)/shard_map/ppermute | solution.py:21
  35.7 0.2 pad_maximum_fusion.1
  35.9 0.3 reverse_select_fusion.1
  36.2 1.8 collective-permute-start.2
  38.1 0.0 copy-done.6
  38.1 11.3 %all-gather = s32[4,1,256]{2,1,0:T(1,128)S(1)} all-gather(s32[1,1,256]{2,1,0:T(1,128)S(1)} %bitcast.41), channel_id=1, replica_groups=mesh['dp'=8,'seq'=4] {'seq'}, dimensions={0}, use_global_device_ids=true | all-gather | bytes 5120 | tf_op jit(solution)/shard_map/all_gather | solution.py:115
  49.4 0.0 copy-done.5
  49.4 8.4 %all-gather.1 = s32[4,1,256]{2,1,0:T(1,128)S(1)} all-gather(s32[1,1,256]{2,1,0:T(1,128)S(1)} %bitcast.40), channel_id=1, replica_groups=mesh['dp'=8,'seq'=4] {'seq'}, dimensions={0}, use_global_device_ids=true | all-gather | bytes 5120 | tf_op jit(solution)/shard_map/all_gather | solution.py:116
  57.9 4.3 %scatter_custom_fusion = s32[128]{0:T(128)S(1)} fusion(s32[1024]{0:T(1024)S(1)} %compare_select_fusion, s32[1024]{0:T(1024)S(1)} %iota.3, s32[]{:T(128)} %constant.74.clone.1), kind=kCustom, calls=%fused_computation.77 | custom fusion | bytes 516 | tf_op jit(solution)/shard_map/scatter | solution.py:128
  62.2 0.0 copy-done.4
  62.2 20.3 %all_gather.26 = bf16[1024,128]{1,0:T(8,128)(2,1)S(1)} all-gather(bf16[128,128]{1,0:T(8,128)(2,1)S(1)} %copy-done.4), channel_id=1, replica_groups=mesh['dp'=8,'seq'=4] {'dp'}, dimensions={0}, use_global_device_ids=true | all-gather | bytes 294912 | tf_op jit(solution)/shard_map/all_gather | solution.py:112
  82.5 0.0 copy-done.1
  82.5 9.7 %all_gather.25 = bf16[1792,128]{1,0:T(8,128)(2,1)S(1)} all-gather(bf16[224,128]{1,0:T(8,128)(2,1)S(1)} %copy-done.1), channel_id=1, replica_groups=mesh['dp'=8,'seq'=4] {'dp'}, dimensions={0}, use_global_device_ids=true | all-gather | bytes 516096 | tf_op jit(solution)/shard_map/all_gather | solution.py:111
  92.2 0.0 collective-permute-done.2
  92.2 1.9 pad_maximum_fusion
  94.1 2.6 reverse_select_fusion
  96.7 3.9 %gather_fusion = bf16[128,1792]{1,0:T(8,128)(2,1)S(1)} fusion(bf16[1024,1792]{1,0:T(8,128)(2,1)} %all-gather.6.cloned.1.call-done, s32[1024]{0:T(1024)S(1)} %pad_clamp_fusion.1), kind=kCustom, calls=%fused_computation | custom fusion | bytes 918016 | tf_op jit(solution)/shard_map/jit(_take)/gather | solution.py:130
  100.6 0.3 fusion.18
  100.9 0.0 copy-done.3
  100.9 0.4 convolution_convert_fusion.1
  101.3 18.3 %all-gather.8.cloned.1.call-done = bf16[1792,1024]{1,0:T(8,128)(2,1)} async-done(((bf16[224,1024]{1,0:T(8,128)(2,1)}), bf16[1792,1024]{1,0:T(8,128)(2,1)}) %all-gather.8.cloned.1.call-update) | async-done | bytes 3670032 | tf_op jit(solution)/shard_map/all_gather | solution.py:109
  119.5 2.7 fusion.39
  122.3 0.0 copy-start
  122.3 0.0 copy-start.2
  122.3 3.0 %multiply_reduce_fusion = (f32[128]{0:T(128)S(1)}, f32[128,1792]{1,0:T(8,128)S(1)}) fusion(bf16[1024,1792]{1,0:T(8,128)(2,1)} %bitcast.31, f32[128,1024]{1,0:T(8,128)S(1)} %fusion.39, bf16[128,128]{1,0:T(8,128)(2,1)S(1)} %convolution_convert_fusion.1, bf16[1024,128]{1,0:T(8,128)(2,1)S(1)} %all_gather.26), kind=kOutput, calls=%fused_computation.42 | convolution fusion | flops 504037248 | bytes 5407232 | tf_op jit(solution)/shard_map/dot_general | solution.py:65
  125.3 0.0 copy-done
  125.3 0.0 copy-done.2
  125.3 1.1 fusion.10
  126.4 3.4 %convolution_convert_fusion = bf16[128,1024]{1,0:T(8,128)(2,1)S(1)} fusion(bf16[1024,1792]{1,0:T(8,128)(2,1)} %bitcast.32, bf16[128,1792]{1,0:T(8,128)(2,1)S(1)} %copy-done, f32[128,1792]{1,0:T(8,128)S(1)} %get-tuple-element.9, f32[128]{0:T(128)S(1)} %broadcast_multiply_fusion.1, f32[1792]{0:T(1024)S(1)} %copy-done.2, f32[128]{0:T(128)S(1)} %add_rsqrt_fusion), kind=kOutput, calls=%fused_computation.20 | convolution fusion | flops 471498752 | bytes 5316608 | tf_op jit(solution)/shard_map/dot_general | solution.py:33
  129.8 0.2 convolution_convert_fusion.2
  130.0 1.2 fusion.1
  131.2 0.0 reduce-scatter.7.cloned.1.call-update
  131.2 0.0 reduce-scatter.9.cloned.1.call-start
  131.2 1.0 fusion.6
  132.2 0.0 reduce-scatter.9.cloned.1.call-update
  132.2 0.0 reduce-scatter.13.cloned.1.call-start
  132.3 3.4 %fusion.41 = f32[128,1792]{1,0:T(8,128)S(1)} fusion(bf16[128,1024]{1,0:T(8,128)(2,1)S(1)} %convolution_convert_fusion, bf16[1792,1024]{1,0:T(8,128)(2,1)} %all-gather.8.cloned.1.call-done), kind=kOutput, calls=%fused_computation.80 | convolution fusion | flops 469762048 | bytes 4849664 | tf_op jit(solution)/shard_map/dot_general | solution.py:33
  135.7 0.4 fusion.15
  136.1 16.3 %reduce-scatter.7.cloned.1.call-done = bf16[1792,32]{0,1:T(8,128)(2,1)} async-done(((bf16[1792,128]{0,1:T(8,128)(2,1)}), bf16[1792,32]{0,1:T(8,128)(2,1)}) %reduce-scatter.7.cloned.1.call-update) | async-done | bytes 114704 | tf_op jit(solution)/shard_map/reduce_scatter | solution.py:148
  152.4 2.0 copy.14
  154.4 0.0 reduce-scatter.13.cloned.1.call-update
  154.4 0.0 all-gather.10.cloned.1.call-start
  154.5 1.3 fusion.13
  155.8 0.0 all-gather.10.cloned.1.call-update
  155.9 0.0 reduce-scatter.11.cloned.1.call-start
  156.0 16.7 %reduce-scatter.9.cloned.1.call-done = bf16[1024,32]{0,1:T(8,128)(2,1)} async-done(((bf16[1024,128]{0,1:T(8,128)(2,1)}), bf16[1024,32]{0,1:T(8,128)(2,1)}) %reduce-scatter.9.cloned.1.call-update) | async-done | bytes 65552 | tf_op jit(solution)/shard_map/reduce_scatter | solution.py:151
  172.7 1.5 convert_element_type.55
  174.2 0.0 reduce-scatter.11.cloned.1.call-update
  174.2 35.8 %reduce-scatter.13.cloned.1.call-done = f32[224,32]{1,0:T(8,128)} async-done(((f32[1792,32]{1,0:T(8,128)}), f32[224,32]{1,0:T(8,128)}) %reduce-scatter.13.cloned.1.call-update) | async-done | bytes 28688
  210.0 1.6 copy.15
  211.6 41.3 %all-gather.10.cloned.1.call-done = bf16[512,1792]{1,0:T(8,128)(2,1)} async-done(((bf16[128,1792]{1,0:T(8,128)(2,1)}), bf16[512,1792]{1,0:T(8,128)(2,1)}) %all-gather.10.cloned.1.call-update) | async-done | bytes 1835024 | tf_op jit(solution)/shard_map/all_gather | solution.py:141
  252.9 3.9 %gather_fusion.1 = bf16[256,1792]{1,0:T(8,128)(2,1)S(1)} fusion(bf16[512,1792]{1,0:T(8,128)(2,1)} %all-gather.10.cloned.1.call-done, s32[1024]{0:T(1024)S(1)} %pad_clamp_fusion), kind=kCustom, calls=%fused_computation.1 | custom fusion | bytes 1836032 | tf_op jit(solution)/shard_map/jit(_take)/gather | solution.py:142
  256.7 1.1 select_select_fusion
  257.9 30.8 %reduce-scatter.11.cloned.1.call-done = f32[128,32]{0,1:T(8,128)} async-done(((f32[1024,32]{0,1:T(8,128)}), f32[128,32]{0,1:T(8,128)}) %reduce-scatter.11.cloned.1.call-update) | async-done | bytes 16400 | tf_op jit(solution)/shard_map/reduce_scatter | solution.py:157
  (21 shorter events, 0.1 us)
Async XLA Ops:
  7.2 89.6 %all-gather.6.cloned.1.call-start = ((), (), s32[]{:S(2)}) async-start(), calls=%async_computation.4 | async-start | bytes 4587520 | tf_op jit(solution)/shard_map/all_gather | solution.py:124
  7.9 111.6 %all-gather.8.cloned.1.call-start = ((), (), s32[]{:S(2)}) async-start(), calls=%async_computation.5 | async-start | bytes 4128768 | tf_op jit(solution)/shard_map/all_gather | solution.py:109
  8.6 143.7 %reduce-scatter.7.cloned.1.call-start = ((), (), s32[]{:S(2)}) async-start(), calls=%async_computation.7 | async-start | bytes 573440 | tf_op jit(solution)/shard_map/reduce_scatter | solution.py:148
  8.7 2.2 collective-permute-start
  12.1 23.6 %collective-permute-start.1 = (bf16[2,128,1792]{2,1,0:T(8,128)(2,1)S(1)}, bf16[2,128,1792]{2,1,0:T(8,128)(2,1)S(1)}, u32[]{:S(2)}, u32[]{:S(2)}) collective-permute-start(bf16[2,128,1792]{2,1,0:T(8,128)(2,1)S(1)} %get-tuple-element.7), channel_id=1, source_target_pairs={{0,8},{4,12},{8,0},{12,4},{16,24},{20,28},{24,16},{28,20},{1,9},{5... | collective-permute-start | bytes 2752520 | tf_op jit(solution)/shard_map/ppermute | solution.py:21
  35.7 2.3 copy-start.6
  35.7 13.7 %copy-start.5 = (s32[256]{0:T(256)S(1)}, s32[256]{0:T(256)}, u32[]{:S(2)}) copy-start(s32[256]{0:T(256)} %param.12) | copy-start | bytes 3076
  35.7 26.5 %copy-start.4 = (bf16[128,128]{1,0:T(8,128)(2,1)S(1)}, bf16[128,128]{1,0:T(8,128)(2,1)}, u32[]{:S(2)}) copy-start(bf16[128,128]{1,0:T(8,128)(2,1)} %param.16) | copy-start | bytes 98308
  35.7 46.8 %copy-start.1 = (bf16[224,128]{1,0:T(8,128)(2,1)S(1)}, bf16[224,128]{1,0:T(8,128)(2,1)}, u32[]{:S(2)}) copy-start(bf16[224,128]{1,0:T(8,128)(2,1)} %param.15) | copy-start | bytes 172036
  36.2 56.0 %collective-permute-start.2 = (bf16[4,128,1792]{2,1,0:T(8,128)(2,1)S(1)}, bf16[4,128,1792]{2,1,0:T(8,128)(2,1)}, u32[]{:S(2)}, u32[]{:S(2)}) collective-permute-start(bf16[4,128,1792]{2,1,0:T(8,128)(2,1)S(1)} %bitcast.33), channel_id=1, source_target_pairs={{0,16},{4,20},{8,24},{12,28},{16,0},{20,4},{24,8},{28,12},{1,17},{... | collective-permute-start | bytes 5505032 | tf_op jit(solution)/shard_map/ppermute | solution.py:21
  96.7 4.2 %copy-start.3 = (f32[1792]{0:T(1024)S(1)}, f32[1792]{0:T(1024)}, u32[]{:S(2)}) copy-start(f32[1792]{0:T(1024)} %param.17) | copy-start | bytes 21508
  122.3 3.0 %copy-start = (bf16[128,1792]{1,0:T(8,128)(2,1)S(1)}, bf16[128,1792]{1,0:T(8,128)(2,1)}, u32[]{:S(2)}) copy-start(bf16[128,1792]{1,0:T(8,128)(2,1)} %param.19) | copy-start | bytes 1376260
  122.3 3.0 %copy-start.2 = (f32[1792]{0:T(1024)S(1)}, f32[1792]{0:T(1024)}, u32[]{:S(2)}) copy-start(f32[1792]{0:T(1024)} %param.18) | copy-start | bytes 21508
  131.2 41.5 %reduce-scatter.9.cloned.1.call-start = ((), (), s32[]{:S(2)}) async-start(), calls=%async_computation.8 | async-start | bytes 327680 | tf_op jit(solution)/shard_map/reduce_scatter | solution.py:151
  132.2 77.8 %reduce-scatter.13.cloned.1.call-start = ((), (), s32[]{:S(2)}) async-start(), calls=%async_computation.10 | async-start | bytes 1032192
  154.4 98.4 %all-gather.10.cloned.1.call-start = ((), (), s32[]{:S(2)}) async-start(), calls=%async_computation.6 | async-start | bytes 2293760 | tf_op jit(solution)/shard_map/all_gather | solution.py:141
  155.9 132.8 %reduce-scatter.11.cloned.1.call-start = ((), (), s32[]{:S(2)}) async-start(), calls=%async_computation.9 | async-start | bytes 147456 | tf_op jit(solution)/shard_map/reduce_scatter | solution.py:157
Sparse Core Ops, SparseCore 0:
  9.6 74.8 all-gather.5
  86.4 33.1 all-gather.7
  131.3 21.0 reduce-scatter.6
  154.6 18.0 reduce-scatter.8
  176.3 33.6 reduce-scatter.12
  211.4 41.3 all-gather.9
  256.4 32.2 reduce-scatter.10
